TPU v7x, 256 devices: a whole 4x4x8 slice. The times are simulated.
256 devices in a mesh: row: 16 (over x_lo, y, core), col: 16 (over z, x_hi).
Axes of the slice: x: 4 (x_hi: 2, x_lo: 2; x = x_hi * 2 + x_lo), y: 4, z: 8, core: 2. Of those that a mesh axis runs over, the one named last changes fastest.
Arguments:
- block_vecs: float32 [16, 131072], P(None, ('col', 'row')), may hold values from -130 to 130
- direction: float32 [16, 131072], P(None, ('col', 'row')), may hold values from -130 to 130
- blocks: bfloat16 [1024, 32, 128, 128], P('col', 'row'), may hold values from 0 to 4
- block_cols: int32 [1024, 32], P('col', 'row'), may hold values from 0 to 1023, as said below
- live_counts: int32 [1024, 16], P('col', 'row'), may hold values from 1 to 2, as said below
Outputs:
- x_next: float32 [16, 131072], P(None, ('col', 'row'))
- reduced: float32 [48, 48], replicated
- residual: float32 [16, 131072], P(None, ('col', 'row'))
Inputs may be any that keep to these rules, and one draw needn't show every extreme that they name: `block_cols`: A block column index g in slots 2 * r to 2 * r + 1 of any block row satisfies (g // 4) mod 16 == r. `live_counts`: every block row has 2 live slots in at least one segment.
All inputs are finite; a program needn't handle non-finite values.
Results may differ from a plain program's by a relative error of at most 0.0003.
Values sent between devices are 32-bit elements; how exact they have to be, the bound alone decides.
A program may use at most 64 MiB of HBM per device.

v0:
```python
import math
import jax
import jax.numpy as jnp
from jax import lax
from jax.sharding import PartitionSpec as P

highest = lax.Precision.HIGHEST


def outer(left, right):
    return jnp.dot(left, right.T, precision=highest, preferred_element_type=jnp.float32)


def cholesky_lower(matrix):
    order_small = matrix.shape[0]
    places = jnp.arange(order_small, dtype=jnp.int32)

    def column_step(step, lower):
        pick = (places == step).astype(jnp.float32)
        row_now = jnp.sum(lower * pick[:, None], axis=0)
        column_now = jnp.sum(matrix * pick[None, :], axis=1)
        pivot = jnp.sum(column_now * pick) - jnp.sum(row_now * row_now)
        pivot_root = jnp.sqrt(pivot)
        below = (column_now - jnp.sum(lower * row_now[None, :], axis=1)) / pivot_root
        values = jnp.where(places > step, below, jnp.where(places == step, pivot_root, 0.0))
        return lower + values[:, None] * pick[None, :]

    return lax.fori_loop(0, order_small, column_step, jnp.zeros_like(matrix))


def solve_lower(lower, right):
    order_small = lower.shape[0]
    places = jnp.arange(order_small, dtype=jnp.int32)

    def row_step(step, solved):
        pick = (places == step).astype(jnp.float32)
        row_now = jnp.sum(lower * pick[:, None], axis=0)
        pivot = jnp.sum(row_now * pick)
        right_row = jnp.sum(right * pick[:, None], axis=0)
        value = (right_row - jnp.sum(row_now[:, None] * solved, axis=0)) / pivot
        return solved + pick[:, None] * value[None, :]

    return lax.fori_loop(0, order_small, row_step, jnp.zeros_like(right))


def solve_upper_t(lower, right):
    order_small = lower.shape[0]
    places = jnp.arange(order_small, dtype=jnp.int32)

    def row_step(count, solved):
        step = order_small - 1 - count
        pick = (places == step).astype(jnp.float32)
        column_now = jnp.sum(lower * pick[None, :], axis=1)
        pivot = jnp.sum(column_now * pick)
        right_row = jnp.sum(right * pick[:, None], axis=0)
        value = (right_row - jnp.sum(column_now[:, None] * solved, axis=0)) / pivot
        return solved + pick[:, None] * value[None, :]

    return lax.fori_loop(0, order_small, row_step, jnp.zeros_like(right))


def local_layout(block_cols, live_counts, span_rows, block_size, row_count):
    per_span = span_rows // block_size
    span_index = block_cols // per_span
    local_cols = span_index // row_count * per_span + block_cols % per_span
    slot_count = block_cols.shape[1]
    live_mask = (jnp.arange(slot_count, dtype=jnp.int32)[None, :] < live_counts).astype(jnp.float32)
    return (local_cols, live_mask)


def forward_part(col_panel, blocks, local_cols, live_mask):
    vec_width = col_panel.shape[0]
    block_size = blocks.shape[2]
    col_blocks = col_panel.reshape(vec_width, -1, block_size)
    picked = col_blocks[:, local_cols, :] * live_mask[None, :, :, None]
    forward = jnp.einsum(
        "vbkj,bkij->vbi", picked, blocks, precision=highest, preferred_element_type=jnp.float32
    )
    return 0.5 * forward.reshape(vec_width, -1)


def backward_part(row_panel, col_length, blocks, local_cols, live_mask):
    vec_width = row_panel.shape[0]
    block_size = blocks.shape[2]
    row_blocks = row_panel.reshape(vec_width, -1, block_size)
    backward = (
        jnp.einsum(
            "vbi,bkij->vbkj",
            row_blocks,
            blocks,
            precision=highest,
            preferred_element_type=jnp.float32,
        )
        * live_mask[None, :, :, None]
    )
    spread = jnp.zeros((vec_width, col_length // block_size, block_size), jnp.float32)
    spread = spread.at[:, local_cols.reshape(-1), :].add(
        backward.reshape(vec_width, -1, block_size)
    )
    return 0.5 * spread.reshape(vec_width, -1)


def per_device(block_vecs, direction, blocks, block_cols, live_counts):
    row_count = lax.axis_size("row")
    col_count = lax.axis_size("col")
    vec_width = block_vecs.shape[0]
    span_rows = block_vecs.shape[1]
    order_total = span_rows * row_count * col_count
    col_length = span_rows * col_count
    block_size = blocks.shape[2]
    local_cols, live_mask = local_layout(block_cols, live_counts, span_rows, block_size, row_count)
    paired = jnp.concatenate([block_vecs, direction], axis=0)
    pair_cols = lax.all_gather(paired, "col", axis=1, tiled=True)
    pair_rows = lax.all_gather(paired, "row", axis=1, tiled=True)
    forward = forward_part(pair_cols, blocks, local_cols, live_mask)
    backward = backward_part(pair_rows, col_length, blocks, local_cols, live_mask)
    image_pair = lax.psum_scatter(
        forward, "row", scatter_dimension=1, tiled=True
    ) + lax.psum_scatter(backward, "col", scatter_dimension=1, tiled=True)
    image_x = image_pair[:vec_width]
    image_p = image_pair[vec_width:]
    gram_x, cross_x = lax.psum(
        (outer(block_vecs, block_vecs), outer(block_vecs, image_x)), ("row", "col")
    )
    factor_x = cholesky_lower(gram_x)
    coefficient = solve_upper_t(factor_x, solve_lower(factor_x, cross_x))
    resid = image_x - jnp.dot(
        coefficient.T, block_vecs, precision=highest, preferred_element_type=jnp.float32
    )
    basis = jnp.concatenate([block_vecs, resid, direction], axis=0)
    resid_cols = lax.all_gather(resid, "col", axis=1, tiled=True)
    resid_rows = lax.all_gather(resid, "row", axis=1, tiled=True)
    forward_r = forward_part(resid_cols, blocks, local_cols, live_mask)
    column_x = outer(basis, image_x)
    column_p = outer(basis, image_p)
    backward_r = backward_part(resid_rows, col_length, blocks, local_cols, live_mask)
    image_r = lax.psum_scatter(
        forward_r, "row", scatter_dimension=1, tiled=True
    ) + lax.psum_scatter(backward_r, "col", scatter_dimension=1, tiled=True)
    column_r = outer(basis, image_r)
    gram_apply = jnp.concatenate([column_x, column_r, column_p], axis=1)
    gram_basis, gram_apply = lax.psum((outer(basis, basis), gram_apply), ("row", "col"))
    factor = cholesky_lower(gram_basis)
    halfway = solve_lower(factor, 0.5 * (gram_apply + gram_apply.T))
    reduced = solve_lower(factor, halfway.T)
    shifted = reduced + 3.0 * jnp.eye(3 * vec_width, dtype=jnp.float32)
    target = jnp.dot(
        shifted, shifted[:, :vec_width], precision=highest, preferred_element_type=jnp.float32
    )
    mixing = solve_upper_t(factor, target)
    fresh = jnp.dot(mixing.T, basis, precision=highest, preferred_element_type=jnp.float32)
    gram_fresh = lax.psum(outer(fresh, fresh), ("row", "col"))
    factor_fresh = cholesky_lower(gram_fresh)
    x_next = math.sqrt(order_total) * solve_lower(factor_fresh, fresh)
    return (x_next, reduced, resid)


def solution(mesh):
    return jax.shard_map(
        per_device,
        mesh=mesh,
        in_specs=(
            P(None, ("col", "row")),
            P(None, ("col", "row")),
            P("col", "row", None, None),
            P("col", "row"),
            P("col", "row"),
        ),
        out_specs=(P(None, ("col", "row")), P(), P(None, ("col", "row"))),
        check_vma=False,
    )
```

profile of v0, /device:TPU:1, one launch (start us, length us, event | category | flops | bytes accessed | tf_op | source)
XLA Modules:
  0.0 1421.3 jit_solution(11187509048310806808)
XLA Ops:
  7.2 0.8 constant_dynamic-update-slice_fusion.1
  8.0 0.8 constant_dynamic-update-slice_fusion
  9.4 0.7 all-gather.3.cloned.1.call-update
  10.2 0.7 fusion.60
  10.9 0.7 compare_select_fusion.9
  11.9 37.2 %all-gather.5.cloned.1.call-done = f32[32,8192]{1,0:T(8,128)} async-done(((f32[32,512]{1,0:T(8,128)}), f32[32,8192]{1,0:T(8,128)}) %all-gather.5.cloned.1.call-update) | async-done | bytes 1048592 | tf_op jit(solution)/shard_map/all_gather | solution.py:114
  49.0 1.4 copy.57
  50.4 4.3 convolution_multiply_fusion
  54.9 5.7 scatter_fusion
  60.6 1.1 copy_bitcast_fusion
  62.0 64.4 %all-gather.3.cloned.1.call-done = f32[32,8192]{1,0:T(8,128)} async-done(((f32[32,512]{1,0:T(8,128)}), f32[32,8192]{1,0:T(8,128)}) %all-gather.3.cloned.1.call-update) | async-done | bytes 1048592 | tf_op jit(solution)/shard_map/all_gather | solution.py:113
  126.4 1.4 copy_bitcast_fusion.2
  127.8 0.8 gather_fusion
  128.6 6.0 fusion.45
  134.6 1.1 copy.69
  135.9 192.4 %reduce-scatter.7.cloned.1.call-done = f32[32,512]{1,0:T(8,128)} async-done(((f32[32,8192]{1,0:T(8,128)}), f32[32,512]{1,0:T(8,128)}) %reduce-scatter.7.cloned.1.call-update) | async-done | bytes 65552 | tf_op jit(solution)/shard_map/reduce_scatter | solution.py:119
  328.3 66.4 %reduce-scatter.5.cloned.1.call-done = f32[32,512]{1,0:T(8,128)} async-done(((f32[32,8192]{1,0:T(8,128)}), f32[32,512]{1,0:T(8,128)}) %reduce-scatter.5.cloned.1.call-update) | async-done | bytes 65552 | tf_op jit(solution)/shard_map/reduce_scatter | solution.py:117
  394.7 0.9 add.271
  395.7 78.8 %all-reduce.1 = (f32[16,16]{0,1:T(8,128)S(1)}, f32[16,16]{1,0:T(8,128)S(1)}) all-reduce(f32[16,16]{0,1:T(8,128)S(1)} %convolution_bitcast_fusion.1, f32[16,16]{1,0:T(8,128)S(1)} %fusion.72), channel_id=1, replica_groups=mesh['row'=16,'col'=16] {'row','col'}, use_global_device_ids=true, to_apply=%region_11.12 | all-reduce | flops 512 | bytes 4096 | tf_op jit(solution)/shard_map/psum | solution.py:122
  474.5 37.0 %while.135 = (s32[]{:T(128)}, f32[16,16]{1,0:T(8,128)S(1)}, f32[16,16]{1,0:T(8,128)S(1)}, s32[]{:T(128)}, s32[]{:T(128)}) while((s32[]{:T(128)}, f32[16,16]{1,0:T(8,128)S(1)}, f32[16,16]{1,0:T(8,128)S(1)}, s32[]{:T(128)}, s32[]{:T(128)}) %tuple.302), condition=%wide.region_10.11_spmd.clone.clone, body=%wide.region_4.10_spmd.clone.clone.sunk | while | flops 2978 | bytes 6069 | solution.py:28
  511.6 24.3 %while.129 = (s32[]{:T(128)}, f32[16,16]{1,0:T(8,128)S(1)}, f32[16,16]{1,0:T(8,128)S(1)}, f32[16,16]{1,0:T(8,128)S(1)}, s32[]{:T(128)}, /*index=5*/s32[]{:T(128)}) while((s32[]{:T(128)}, f32[16,16]{1,0:T(8,128)S(1)}, f32[16,16]{1,0:T(8,128)S(1)}, f32[16,16]{1,0:T(8,128)S(1)}, s32[]{:T(128)}, /*index=5*/s32[]{:T(128)}) %tuple.305), condition=%wide.region_17.18_spmd.clone, body=%wide.region_12.17_spmd.clone.sunk | while | flops 2626 | bytes 5984 | solution.py:43
  535.9 24.8 %while.130 = (s32[]{:T(128)}, f32[16,16]{1,0:T(8,128)S(1)}, f32[16,16]{1,0:T(8,128)S(1)}, f32[16,16]{1,0:T(8,128)S(1)}, s32[]{:T(128)}, /*index=5*/s32[]{:T(128)}, s32[]{:T(128)}) while((s32[]{:T(128)}, f32[16,16]{1,0:T(8,128)S(1)}, f32[16,16]{1,0:T(8,128)S(1)}, f32[16,16]{1,0:T(8,128)S(1)}, s32[]{:T(128)}, ...), condition=%wide.region_23.24_spmd.clone, body=%wide.region_18.23_spmd.clone.sunk | while | flops 2627 | bytes 6004 | solution.py:59
  560.9 19.6 %all_gather.15 = f32[16,8192]{1,0:T(8,128)S(1)} all-gather(f32[16,512]{1,0:T(8,128)S(1)} %convolution_subtract_fusion), channel_id=1, replica_groups=mesh['row'=16,'col'=16] {'row'}, dimensions={1}, use_global_device_ids=true | all-gather | bytes 557056 | tf_op jit(solution)/shard_map/all_gather | solution.py:132
  580.6 3.8 convolution_multiply_fusion.1
  584.5 5.2 scatter_fusion.1
  589.7 0.8 copy_bitcast_fusion.3
  590.6 34.6 %all_gather.14 = f32[16,8192]{1,0:T(8,128)S(1)} all-gather(f32[16,512]{1,0:T(8,128)S(1)} %convolution_subtract_fusion), channel_id=1, replica_groups=mesh['row'=16,'col'=16] {'col'}, dimensions={1}, use_global_device_ids=true | all-gather | bytes 557056 | tf_op jit(solution)/shard_map/all_gather | solution.py:131
  625.3 0.8 gather_fusion.1
  626.0 5.2 fusion.49
  631.2 0.8 copy.70
  632.8 145.4 %reduce-scatter.11.cloned.1.call-done = f32[16,512]{1,0:T(8,128)} async-done(((f32[16,8192]{1,0:T(8,128)}), f32[16,512]{1,0:T(8,128)}) %reduce-scatter.11.cloned.1.call-update) | async-done | bytes 32784 | tf_op jit(solution)/shard_map/reduce_scatter | solution.py:139
  778.1 65.7 %reduce-scatter.9.cloned.1.call-done = f32[16,512]{1,0:T(8,128)} async-done(((f32[16,8192]{1,0:T(8,128)}), f32[16,512]{1,0:T(8,128)}) %reduce-scatter.9.cloned.1.call-update) | async-done | bytes 32784 | tf_op jit(solution)/shard_map/reduce_scatter | solution.py:137
  843.8 0.9 fusion.58
  844.8 79.4 %all-reduce = (f32[48,48]{0,1:T(8,128)S(1)}, f32[48,48]{1,0:T(8,128)S(1)}) all-reduce(f32[48,48]{0,1:T(8,128)S(1)} %pad_maximum_fusion.1, f32[48,48]{1,0:T(8,128)S(1)} %fusion.70), channel_id=1, replica_groups=mesh['row'=16,'col'=16] {'row','col'}, use_global_device_ids=true, to_apply=%region_35.36 | all-reduce | flops 4608 | bytes 36864 | tf_op jit(solution)/shard_map/psum | solution.py:142
  924.3 111.3 %while.136 = (s32[]{:T(128)}, f32[48,48]{1,0:T(8,128)S(1)}, f32[48,48]{1,0:T(8,128)S(1)}, s32[]{:T(128)}, s32[]{:T(128)}) while((s32[]{:T(128)}, f32[48,48]{1,0:T(8,128)S(1)}, f32[48,48]{1,0:T(8,128)S(1)}, s32[]{:T(128)}, s32[]{:T(128)}) %tuple.311), condition=%wide.region_31.32_spmd.clone.clone, body=%wide.region_25.31_spmd.clone.clone.sunk | while | flops 25826 | bytes 48693 | solution.py:28
  1035.6 79.4 %while.131 = (s32[]{:T(128)}, f32[48,48]{1,0:T(8,128)S(1)}, f32[48,48]{1,0:T(8,128)S(1)}, f32[48,48]{1,0:T(8,128)S(1)}, s32[]{:T(128)}, /*index=5*/s32[]{:T(128)}) while((s32[]{:T(128)}, f32[48,48]{1,0:T(8,128)S(1)}, f32[48,48]{1,0:T(8,128)S(1)}, f32[48,48]{1,0:T(8,128)S(1)}, s32[]{:T(128)}, /*index=5*/s32[]{:T(128)}) %tuple.314), condition=%wide.region_41.42_spmd.clone, body=%wide.region_36.41_spmd.clone.sunk | while | flops 23234 | bytes 48480 | solution.py:43
  1038.1 0.7 subtract_divide_fusion.14
  1048.1 0.7 subtract_divide_fusion.14
  1049.7 0.7 subtract_divide_fusion.14
  1058.0 0.7 subtract_divide_fusion.14
  1059.6 0.7 subtract_divide_fusion.14
  1069.6 0.7 subtract_divide_fusion.14
  1079.5 0.7 subtract_divide_fusion.14
  1081.2 0.7 subtract_divide_fusion.14
  1089.4 0.7 subtract_divide_fusion.14
  1091.1 0.7 subtract_divide_fusion.14
  1101.0 0.7 subtract_divide_fusion.14
  1110.9 0.7 subtract_divide_fusion.14
  1112.6 0.7 subtract_divide_fusion.14
  1115.1 79.4 %while.132 = (s32[]{:T(128)}, f32[48,48]{1,0:T(8,128)S(1)}, f32[48,48]{1,0:T(8,128)S(1)}, f32[48,48]{1,0:T(8,128)S(1)}, s32[]{:T(128)}, /*index=5*/s32[]{:T(128)}) while((s32[]{:T(128)}, f32[48,48]{1,0:T(8,128)S(1)}, f32[48,48]{1,0:T(8,128)S(1)}, f32[48,48]{1,0:T(8,128)S(1)}, s32[]{:T(128)}, /*index=5*/s32[]{:T(128)}) %tuple.344), condition=%wide.region_47.48_spmd.clone, body=%wide.region_42.47_spmd.clone.sunk | while | flops 23234 | bytes 48480 | solution.py:43
  1124.3 0.7 subtract_divide_fusion.15
  1134.2 0.7 subtract_divide_fusion.15
  1135.8 0.7 subtract_divide_fusion.15
  1144.1 0.7 subtract_divide_fusion.15
  1145.8 0.7 subtract_divide_fusion.15
  1155.7 0.7 subtract_divide_fusion.15
  1165.6 0.7 subtract_divide_fusion.15
  1167.3 0.7 subtract_divide_fusion.15
  1175.6 0.7 subtract_divide_fusion.15
  1177.2 0.7 subtract_divide_fusion.15
  1194.8 81.8 %while.133 = (s32[]{:T(128)}, f32[48,16]{0,1:T(8,128)S(1)}, f32[48,16]{0,1:T(8,128)S(1)}, f32[48,48]{1,0:T(8,128)S(1)}, s32[]{:T(128)}, /*index=5*/s32[]{:T(128)}, s32[]{:T(128)}) while((s32[]{:T(128)}, f32[48,16]{0,1:T(8,128)S(1)}, f32[48,16]{0,1:T(8,128)S(1)}, f32[48,48]{1,0:T(8,128)S(1)}, s32[]{:T(128)}, ...), condition=%wide.region_53.54_spmd.clone, body=%wide.region_48.53_spmd.clone.sunk | while | flops 10947 | bytes 23348 | solution.py:59
  1276.8 73.6 %psum.39 = f32[16,16]{1,0:T(8,128)S(1)} all-reduce(f32[16,16]{1,0:T(8,128)S(1)} %fusion.73), channel_id=1, replica_groups=mesh['row'=16,'col'=16] {'row','col'}, use_global_device_ids=true, to_apply=%region_54.55 | all-reduce | flops 256 | bytes 2048 | tf_op jit(solution)/shard_map/psum | solution.py:152
  1350.5 37.0 %while.137 = (s32[]{:T(128)}, f32[16,16]{1,0:T(8,128)S(1)}, f32[16,16]{1,0:T(8,128)S(1)}, s32[]{:T(128)}, s32[]{:T(128)}) while((s32[]{:T(128)}, f32[16,16]{1,0:T(8,128)S(1)}, f32[16,16]{1,0:T(8,128)S(1)}, s32[]{:T(128)}, s32[]{:T(128)}) %tuple.323), condition=%wide.region_61.62_spmd.clone.clone, body=%wide.region_55.61_spmd.clone.clone.sunk | while | flops 2978 | bytes 6069 | solution.py:28
  1387.5 26.3 %while.134 = (s32[]{:T(128)}, f32[16,512]{1,0:T(8,128)S(1)}, f32[16,512]{1,0:T(8,128)S(1)}, f32[16,16]{1,0:T(8,128)S(1)}, s32[]{:T(128)}, /*index=5*/s32[]{:T(128)}) while((s32[]{:T(128)}, f32[16,512]{1,0:T(8,128)S(1)}, f32[16,512]{1,0:T(8,128)S(1)}, f32[16,16]{1,0:T(8,128)S(1)}, s32[]{:T(128)}, /*index=5*/s32[]{:T(128)}) %tuple.326), condition=%wide.region_67.68_spmd.clone, body=%wide.region_62.67_spmd.clone.sunk | while | flops 66114 | bytes 144928 | solution.py:43
  (1666 shorter events, 382.5 us)
Async XLA Ops:
  7.2 41.9 %all-gather.5.cloned.1.call-start = ((), (), s32[]{:S(2)}) async-start(), calls=%async_computation.6 | async-start | bytes 1114112 | tf_op jit(solution)/shard_map/all_gather | solution.py:114
  8.7 0.6 copy-start.4
  9.4 117.1 %all-gather.3.cloned.1.call-start = ((), (), s32[]{:S(2)}) async-start(), calls=%async_computation.4 | async-start | bytes 1114112 | tf_op jit(solution)/shard_map/all_gather | solution.py:113
  10.1 318.2 %reduce-scatter.7.cloned.1.call-start = ((), (), s32[]{:S(2)}) async-start(), calls=%async_computation.7 | async-start | bytes 1114112 | tf_op jit(solution)/shard_map/reduce_scatter | solution.py:119
  61.7 333.0 %reduce-scatter.5.cloned.1.call-start = ((), (), s32[]{:S(2)}) async-start(), calls=%async_computation.5 | async-start | bytes 1114112 | tf_op jit(solution)/shard_map/reduce_scatter | solution.py:117
  134.6 1.2 copy-start.1
  135.7 642.4 %reduce-scatter.11.cloned.1.call-start = ((), (), s32[]{:S(2)}) async-start(), calls=%async_computation.9 | async-start | bytes 557056 | tf_op jit(solution)/shard_map/reduce_scatter | solution.py:139
  560.9 715.6 %copy-start.2 = (f32[16,512]{1,0:T(8,128)}, f32[16,512]{1,0:T(8,128)S(1)}, u32[]{:S(2)}) copy-start(f32[16,512]{1,0:T(8,128)S(1)} %convolution_subtract_fusion) | copy-start | bytes 98308
  590.5 253.3 %reduce-scatter.9.cloned.1.call-start = ((), (), s32[]{:S(2)}) async-start(), calls=%async_computation.8 | async-start | bytes 557056 | tf_op jit(solution)/shard_map/reduce_scatter | solution.py:137
  626.0 6.1 copy-start.3
  1194.5 219.9 %copy-start = (f32[48,48]{1,0:T(8,128)}, f32[48,48]{1,0:T(8,128)S(1)}, u32[]{:S(2)}) copy-start(f32[48,48]{1,0:T(8,128)S(1)} %get-tuple-element.811) | copy-start | bytes 27652
Sparse Core Ops, SparseCore 0:
  9.8 39.1 all-gather.4
  51.6 74.7 all-gather.2
  130.3 198.0 reduce-scatter.6
  330.7 63.9 reduce-scatter.4
  590.6 187.4 reduce-scatter.10
  780.5 63.2 reduce-scatter.8
where the time goes:
time: 1430 us; the launch traced here: 1420 us
  waiting for transfers between devices  572 us (40%)
  other arithmetic  410 us (29%)
  blocking collectives  286 us (20%)
  loops' own time  107 us (7%)
  matrix products  21.8 us (2%)
  between operations  14.4 us (1%)
    reduce_scatter x1, waiting for transfers between devices, per_device(): lax.psum_scatter(backward, 'col', scatter_dimension=1, tiled=True)  192 us
    reduce_scatter x1, waiting for transfers between devices, per_device(): lax.psum_scatter(backward_r, 'col', scatter_dimension=1, tiled=True)  145 us
    another operation x3, loops' own time, cholesky_lower(): return lax.fori_loop(0, order_small, column_step, jnp.zeros_like(matrix))  105 us
    div x128, other arithmetic, row_step(): value = (right_row - jnp.sum(row_now[:, None] * solved, axis=0)) / pivot  87.9 us
    reduce_sum x128, other arithmetic, row_step(): pivot = jnp.sum(row_now * pick)  85.7 us
    psum x1, blocking collectives, per_device(): lax.psum((outer(basis, basis), gram_apply), ('row', 'col'))  79.4 us
    psum x1, blocking collectives, per_device(): lax.psum((outer(block_vecs, block_vecs), outer(block_vecs, image_x)), ('r...  78.8 us
    psum x1, blocking collectives, per_device(): gram_fresh = lax.psum(outer(fresh, fresh), ('row', 'col'))  73.6 us
  transfers between devices with their start and end apart: 6, of which 6 were waited for; matrix products, arithmetic and copies ran while one was open for 2% of the time, Pallas kernels for 0%

commit v1 on v0

--- a/solution.py
+++ b/solution.py
@@ -149,7 +149,7 @@
     )
     mixing = solve_upper_t(factor, target)
     fresh = jnp.dot(mixing.T, basis, precision=highest, preferred_element_type=jnp.float32)
-    gram_fresh = lax.psum(outer(fresh, fresh), ("row", "col"))
+    gram_fresh = jnp.sum(lax.all_gather(outer(fresh, fresh), ("row", "col")), axis=0)
     factor_fresh = cholesky_lower(gram_fresh)
     x_next = math.sqrt(order_total) * solve_lower(factor_fresh, fresh)
     return (x_next, reduced, resid)

time: 1430 us -> 1980 us (1.38)
  blocking collectives: 286 us -> 826 us
    all_gather x0 -> x1, blocking collectives: none -> 614 us  [per_device(): lax.all_gather(outer(fresh, fresh), ('row', 'col'))]
    psum x1 -> x0, blocking collectives: 73.6 us -> none  [per_device(): gram_fresh = lax.psum(outer(fresh, fresh), ('row', 'col'))]
where the time goes in v1:
time: 1980 us; the launch traced here: 1960 us
  blocking collectives  826 us (42%)
  waiting for transfers between devices  572 us (29%)
  other arithmetic  410 us (21%)
  loops' own time  107 us (5%)
  matrix products  21.8 us (1%)
    all_gather x1, blocking collectives, per_device(): lax.all_gather(outer(fresh, fresh), ('row', 'col'))  614 us
    reduce_scatter x1, waiting for transfers between devices, per_device(): lax.psum_scatter(backward, 'col', scatter_dimension=1, tiled=True)  192 us
    reduce_scatter x1, waiting for transfers between devices, per_device(): lax.psum_scatter(backward_r, 'col', scatter_dimension=1, tiled=True)  145 us
    another operation x3, loops' own time, cholesky_lower(): return lax.fori_loop(0, order_small, column_step, jnp.zeros_like(matrix))  105 us
    div x128, other arithmetic, row_step(): value = (right_row - jnp.sum(row_now[:, None] * solved, axis=0)) / pivot  87.9 us
    reduce_sum x128, other arithmetic, row_step(): pivot = jnp.sum(row_now * pick)  85.7 us
    psum x1, blocking collectives, per_device(): lax.psum((outer(basis, basis), gram_apply), ('row', 'col'))  79.4 us
    psum x1, blocking collectives, per_device(): lax.psum((outer(block_vecs, block_vecs), outer(block_vecs, image_x)), ('r...  78.8 us
  transfers between devices with their start and end apart: 6, of which 6 were waited for; matrix products, arithmetic and copies ran while one was open for 2% of the time, Pallas kernels for 0%

profile of v1, /device:TPU:1, one launch (start us, length us, event | category | flops | bytes accessed | tf_op | source)
XLA Modules:
  0.0 1962.0 jit_solution(1395994409619123963)
XLA Ops:
  7.2 0.8 constant_dynamic-update-slice_fusion.1
  8.0 0.8 constant_dynamic-update-slice_fusion
  9.4 0.7 all-gather.4.cloned.1.call-update
  10.2 0.7 fusion.60
  10.9 0.7 compare_select_fusion.9
  11.9 37.2 %all-gather.6.cloned.1.call-done = f32[32,8192]{1,0:T(8,128)} async-done(((f32[32,512]{1,0:T(8,128)}), f32[32,8192]{1,0:T(8,128)}) %all-gather.6.cloned.1.call-update) | async-done | bytes 1048592 | tf_op jit(solution)/shard_map/all_gather | solution.py:114
  49.0 1.4 copy.57
  50.4 4.3 convolution_multiply_fusion
  54.9 5.7 scatter_fusion
  60.6 1.1 copy_bitcast_fusion
  62.0 64.4 %all-gather.4.cloned.1.call-done = f32[32,8192]{1,0:T(8,128)} async-done(((f32[32,512]{1,0:T(8,128)}), f32[32,8192]{1,0:T(8,128)}) %all-gather.4.cloned.1.call-update) | async-done | bytes 1048592 | tf_op jit(solution)/shard_map/all_gather | solution.py:113
  126.4 1.4 copy_bitcast_fusion.2
  127.8 0.8 gather_fusion
  128.6 6.0 fusion.45
  134.6 1.1 copy.69
  135.9 192.4 %reduce-scatter.7.cloned.1.call-done = f32[32,512]{1,0:T(8,128)} async-done(((f32[32,8192]{1,0:T(8,128)}), f32[32,512]{1,0:T(8,128)}) %reduce-scatter.7.cloned.1.call-update) | async-done | bytes 65552 | tf_op jit(solution)/shard_map/reduce_scatter | solution.py:119
  328.3 66.4 %reduce-scatter.5.cloned.1.call-done = f32[32,512]{1,0:T(8,128)} async-done(((f32[32,8192]{1,0:T(8,128)}), f32[32,512]{1,0:T(8,128)}) %reduce-scatter.5.cloned.1.call-update) | async-done | bytes 65552 | tf_op jit(solution)/shard_map/reduce_scatter | solution.py:117
  394.7 0.9 add.269
  395.7 78.8 %all-reduce.1 = (f32[16,16]{0,1:T(8,128)S(1)}, f32[16,16]{1,0:T(8,128)S(1)}) all-reduce(f32[16,16]{0,1:T(8,128)S(1)} %convolution_bitcast_fusion.1, f32[16,16]{1,0:T(8,128)S(1)} %fusion.72), channel_id=1, replica_groups=mesh['row'=16,'col'=16] {'row','col'}, use_global_device_ids=true, to_apply=%region_11.12 | all-reduce | flops 512 | bytes 4096 | tf_op jit(solution)/shard_map/psum | solution.py:122
  474.5 37.0 %while.135 = (s32[]{:T(128)}, f32[16,16]{1,0:T(8,128)S(1)}, f32[16,16]{1,0:T(8,128)S(1)}, s32[]{:T(128)}, s32[]{:T(128)}) while((s32[]{:T(128)}, f32[16,16]{1,0:T(8,128)S(1)}, f32[16,16]{1,0:T(8,128)S(1)}, s32[]{:T(128)}, s32[]{:T(128)}) %tuple.302), condition=%wide.region_10.11_spmd.clone.clone, body=%wide.region_4.10_spmd.clone.clone.sunk | while | flops 2978 | bytes 6069 | solution.py:28
  511.6 24.3 %while.129 = (s32[]{:T(128)}, f32[16,16]{1,0:T(8,128)S(1)}, f32[16,16]{1,0:T(8,128)S(1)}, f32[16,16]{1,0:T(8,128)S(1)}, s32[]{:T(128)}, /*index=5*/s32[]{:T(128)}) while((s32[]{:T(128)}, f32[16,16]{1,0:T(8,128)S(1)}, f32[16,16]{1,0:T(8,128)S(1)}, f32[16,16]{1,0:T(8,128)S(1)}, s32[]{:T(128)}, /*index=5*/s32[]{:T(128)}) %tuple.305), condition=%wide.region_17.18_spmd.clone, body=%wide.region_12.17_spmd.clone.sunk | while | flops 2626 | bytes 5984 | solution.py:43
  535.9 24.8 %while.130 = (s32[]{:T(128)}, f32[16,16]{1,0:T(8,128)S(1)}, f32[16,16]{1,0:T(8,128)S(1)}, f32[16,16]{1,0:T(8,128)S(1)}, s32[]{:T(128)}, /*index=5*/s32[]{:T(128)}, s32[]{:T(128)}) while((s32[]{:T(128)}, f32[16,16]{1,0:T(8,128)S(1)}, f32[16,16]{1,0:T(8,128)S(1)}, f32[16,16]{1,0:T(8,128)S(1)}, s32[]{:T(128)}, ...), condition=%wide.region_23.24_spmd.clone, body=%wide.region_18.23_spmd.clone.sunk | while | flops 2627 | bytes 6004 | solution.py:59
  560.9 19.6 all_gather.21
  580.6 3.8 convolution_multiply_fusion.1
  584.5 5.2 scatter_fusion.1
  589.7 0.8 copy_bitcast_fusion.3
  590.6 34.6 %all_gather.20 = f32[16,8192]{1,0:T(8,128)S(1)} all-gather(f32[16,512]{1,0:T(8,128)S(1)} %convolution_subtract_fusion), channel_id=1, replica_groups=mesh['row'=16,'col'=16] {'col'}, dimensions={1}, use_global_device_ids=true | all-gather | bytes 557056 | tf_op jit(solution)/shard_map/all_gather | solution.py:131
  625.3 0.8 gather_fusion.1
  626.0 5.2 fusion.49
  631.2 0.8 copy.70
  632.8 145.4 %reduce-scatter.11.cloned.1.call-done = f32[16,512]{1,0:T(8,128)} async-done(((f32[16,8192]{1,0:T(8,128)}), f32[16,512]{1,0:T(8,128)}) %reduce-scatter.11.cloned.1.call-update) | async-done | bytes 32784 | tf_op jit(solution)/shard_map/reduce_scatter | solution.py:139
  778.2 65.7 %reduce-scatter.9.cloned.1.call-done = f32[16,512]{1,0:T(8,128)} async-done(((f32[16,8192]{1,0:T(8,128)}), f32[16,512]{1,0:T(8,128)}) %reduce-scatter.9.cloned.1.call-update) | async-done | bytes 32784 | tf_op jit(solution)/shard_map/reduce_scatter | solution.py:137
  843.9 0.9 fusion.58
  844.9 79.4 %all-reduce = (f32[48,48]{0,1:T(8,128)S(1)}, f32[48,48]{1,0:T(8,128)S(1)}) all-reduce(f32[48,48]{0,1:T(8,128)S(1)} %pad_maximum_fusion.1, f32[48,48]{1,0:T(8,128)S(1)} %fusion.70), channel_id=1, replica_groups=mesh['row'=16,'col'=16] {'row','col'}, use_global_device_ids=true, to_apply=%region_35.36 | all-reduce | flops 4608 | bytes 36864 | tf_op jit(solution)/shard_map/psum | solution.py:142
  924.4 111.3 %while.136 = (s32[]{:T(128)}, f32[48,48]{1,0:T(8,128)S(1)}, f32[48,48]{1,0:T(8,128)S(1)}, s32[]{:T(128)}, s32[]{:T(128)}) while((s32[]{:T(128)}, f32[48,48]{1,0:T(8,128)S(1)}, f32[48,48]{1,0:T(8,128)S(1)}, s32[]{:T(128)}, s32[]{:T(128)}) %tuple.311), condition=%wide.region_31.32_spmd.clone.clone, body=%wide.region_25.31_spmd.clone.clone.sunk | while | flops 25826 | bytes 48693 | solution.py:28
  1035.6 79.4 %while.131 = (s32[]{:T(128)}, f32[48,48]{1,0:T(8,128)S(1)}, f32[48,48]{1,0:T(8,128)S(1)}, f32[48,48]{1,0:T(8,128)S(1)}, s32[]{:T(128)}, /*index=5*/s32[]{:T(128)}) while((s32[]{:T(128)}, f32[48,48]{1,0:T(8,128)S(1)}, f32[48,48]{1,0:T(8,128)S(1)}, f32[48,48]{1,0:T(8,128)S(1)}, s32[]{:T(128)}, /*index=5*/s32[]{:T(128)}) %tuple.314), condition=%wide.region_41.42_spmd.clone, body=%wide.region_36.41_spmd.clone.sunk | while | flops 23234 | bytes 48480 | solution.py:43
  1041.5 0.7 subtract_divide_fusion.14
  1043.1 0.7 subtract_divide_fusion.14
  1051.4 0.7 subtract_divide_fusion.14
  1053.1 0.7 subtract_divide_fusion.14
  1063.0 0.7 subtract_divide_fusion.14
  1072.9 0.7 subtract_divide_fusion.14
  1074.6 0.7 subtract_divide_fusion.14
  1082.9 0.7 subtract_divide_fusion.14
  1084.5 0.7 subtract_divide_fusion.14
  1094.4 0.7 subtract_divide_fusion.14
  1104.4 0.7 subtract_divide_fusion.14
  1106.0 0.7 subtract_divide_fusion.14
  1114.3 0.7 subtract_divide_fusion.14
  1115.1 79.4 %while.132 = (s32[]{:T(128)}, f32[48,48]{1,0:T(8,128)S(1)}, f32[48,48]{1,0:T(8,128)S(1)}, f32[48,48]{1,0:T(8,128)S(1)}, s32[]{:T(128)}, /*index=5*/s32[]{:T(128)}) while((s32[]{:T(128)}, f32[48,48]{1,0:T(8,128)S(1)}, f32[48,48]{1,0:T(8,128)S(1)}, f32[48,48]{1,0:T(8,128)S(1)}, s32[]{:T(128)}, /*index=5*/s32[]{:T(128)}) %tuple.344), condition=%wide.region_47.48_spmd.clone, body=%wide.region_42.47_spmd.clone.sunk | while | flops 23234 | bytes 48480 | solution.py:43
  1130.9 0.7 subtract_divide_fusion.15
  1134.2 0.7 subtract_divide_fusion.15
  1137.5 0.7 subtract_divide_fusion.15
  1140.8 0.7 subtract_divide_fusion.15
  1144.2 0.7 subtract_divide_fusion.15
  1162.3 0.7 subtract_divide_fusion.15
  1165.7 0.7 subtract_divide_fusion.15
  1169.0 0.7 subtract_divide_fusion.15
  1172.3 0.7 subtract_divide_fusion.15
  1175.6 0.7 subtract_divide_fusion.15
  1194.8 81.8 %while.133 = (s32[]{:T(128)}, f32[48,16]{0,1:T(8,128)S(1)}, f32[48,16]{0,1:T(8,128)S(1)}, f32[48,48]{1,0:T(8,128)S(1)}, s32[]{:T(128)}, /*index=5*/s32[]{:T(128)}, s32[]{:T(128)}) while((s32[]{:T(128)}, f32[48,16]{0,1:T(8,128)S(1)}, f32[48,16]{0,1:T(8,128)S(1)}, f32[48,48]{1,0:T(8,128)S(1)}, s32[]{:T(128)}, ...), condition=%wide.region_53.54_spmd.clone, body=%wide.region_48.53_spmd.clone.sunk | while | flops 10947 | bytes 23348 | solution.py:59
  1276.9 614.0 %all-gather = f32[4096,16]{1,0:T(8,128)S(1)} all-gather(f32[16,16]{1,0:T(8,128)S(1)} %fusion.73), channel_id=2, replica_groups=mesh['row'=16,'col'=16] {'row','col'}, dimensions={0}, use_global_device_ids=true | all-gather | bytes 263168 | tf_op jit(solution)/shard_map/all_gather | solution.py:152
  1891.1 37.0 %while.137 = (s32[]{:T(128)}, f32[16,16]{1,0:T(8,128)S(1)}, f32[16,16]{1,0:T(8,128)S(1)}, s32[]{:T(128)}, s32[]{:T(128)}) while((s32[]{:T(128)}, f32[16,16]{1,0:T(8,128)S(1)}, f32[16,16]{1,0:T(8,128)S(1)}, s32[]{:T(128)}, s32[]{:T(128)}) %tuple.323), condition=%wide.region_61.62_spmd.clone.clone, body=%wide.region_55.61_spmd.clone.clone.sunk | while | flops 2978 | bytes 6069 | solution.py:28
  1928.2 26.3 %while.134 = (s32[]{:T(128)}, f32[16,512]{1,0:T(8,128)S(1)}, f32[16,512]{1,0:T(8,128)S(1)}, f32[16,16]{1,0:T(8,128)S(1)}, s32[]{:T(128)}, /*index=5*/s32[]{:T(128)}) while((s32[]{:T(128)}, f32[16,512]{1,0:T(8,128)S(1)}, f32[16,512]{1,0:T(8,128)S(1)}, f32[16,16]{1,0:T(8,128)S(1)}, s32[]{:T(128)}, /*index=5*/s32[]{:T(128)}) %tuple.326), condition=%wide.region_67.68_spmd.clone, body=%wide.region_62.67_spmd.clone.sunk | while | flops 66114 | bytes 144928 | solution.py:43
  (1667 shorter events, 382.7 us)
Async XLA Ops:
  7.2 41.9 %all-gather.6.cloned.1.call-start = ((), (), s32[]{:S(2)}) async-start(), calls=%async_computation.6 | async-start | bytes 1114112 | tf_op jit(solution)/shard_map/all_gather | solution.py:114
  8.7 0.6 copy-start.4
  9.4 117.1 %all-gather.4.cloned.1.call-start = ((), (), s32[]{:S(2)}) async-start(), calls=%async_computation.4 | async-start | bytes 1114112 | tf_op jit(solution)/shard_map/all_gather | solution.py:113
  10.1 318.2 %reduce-scatter.7.cloned.1.call-start = ((), (), s32[]{:S(2)}) async-start(), calls=%async_computation.7 | async-start | bytes 1114112 | tf_op jit(solution)/shard_map/reduce_scatter | solution.py:119
  61.7 333.0 %reduce-scatter.5.cloned.1.call-start = ((), (), s32[]{:S(2)}) async-start(), calls=%async_computation.5 | async-start | bytes 1114112 | tf_op jit(solution)/shard_map/reduce_scatter | solution.py:117
  134.6 1.2 copy-start.1
  135.7 642.5 %reduce-scatter.11.cloned.1.call-start = ((), (), s32[]{:S(2)}) async-start(), calls=%async_computation.9 | async-start | bytes 557056 | tf_op jit(solution)/shard_map/reduce_scatter | solution.py:139
  560.9 715.6 %copy-start.2 = (f32[16,512]{1,0:T(8,128)}, f32[16,512]{1,0:T(8,128)S(1)}, u32[]{:S(2)}) copy-start(f32[16,512]{1,0:T(8,128)S(1)} %convolution_subtract_fusion) | copy-start | bytes 98308
  590.5 253.3 %reduce-scatter.9.cloned.1.call-start = ((), (), s32[]{:S(2)}) async-start(), calls=%async_computation.8 | async-start | bytes 557056 | tf_op jit(solution)/shard_map/reduce_scatter | solution.py:137
  626.0 6.1 copy-start.3
  1194.6 696.6 %copy-start = (f32[48,48]{1,0:T(8,128)}, f32[48,48]{1,0:T(8,128)S(1)}, u32[]{:S(2)}) copy-start(f32[48,48]{1,0:T(8,128)S(1)} %get-tuple-element.811) | copy-start | bytes 27652
Sparse Core Ops, SparseCore 0:
  9.8 39.1 all-gather.5
  51.6 74.7 all-gather.3
  130.3 198.0 reduce-scatter.6
  330.7 63.9 reduce-scatter.4
  590.7 187.4 reduce-scatter.10
  780.5 63.2 reduce-scatter.8
